TPU v7x, 128 devices: a whole 4x4x4 slice. The times are simulated.
128 devices in a mesh: chaos: 8 (over z, core), space: 16 (over x, y).
Axes of the slice: x: 4, y: 4, z: 4, core: 2. Of those that a mesh axis runs over, the one named last changes fastest.
Arguments:
- panels: bfloat16 [216, 48, 2304], P('chaos', 'space'), may hold values from -6 to 6
- mean_field: float32 [48, 2304], P('space'), may hold values from 0.5 to 2
- fluctuations: float32 [6, 48, 2304], P(None, 'space'), may hold values from -1.5 to 1.5
- products: float32 [1218], replicated, may hold values from -4 to 4
- triples: int32 [1218, 3], replicated, may hold values from 0 to 209, as said below
- owner_slot: int32 [210], replicated, may hold values from 0 to 215, as said below
Outputs:
- first_apply: bfloat16 [216, 48, 2304], P('chaos', 'space')
- second_apply: bfloat16 [216, 48, 2304], P('chaos', 'space')
Inputs may be any that keep to these rules, and one draw needn't show every extreme that they name: `triples`: each row (i, j, k) names a nonzero of G_k; i and j are below 210, k below 7; repeated rows add; every chaos coefficient is some row's i and some row's j. `owner_slot`: distinct slots; slot s belongs to the group s // 27 along chaos.
All inputs are finite; a program needn't handle non-finite values.
Results may differ from a plain program's by a relative error of at most 0.007.
Values may be sent and summed in bfloat16 or wider, within the bound.
A program may use at most 64 MiB of HBM per device.

v0:
```python
import jax
import jax.numpy as jnp
from jax import lax
from jax.sharding import PartitionSpec as P

NXY = 48
scale_factor = 0.15


def padded(block, sides, width):
    for axis, dim in sides:
        count = lax.axis_size(axis)
        forward = [(i, i + 1) for i in range(count - 1)]
        backward = [(target, source) for source, target in forward]
        low = lax.ppermute(
            lax.slice_in_dim(block, block.shape[dim] - width, None, axis=dim), axis, forward
        )
        high = lax.ppermute(lax.slice_in_dim(block, 0, width, axis=dim), axis, backward)
        block = jnp.concatenate([low, block, high], axis=dim)
    return block


def shifted(source, offset, inside):
    length_last = source.shape[-1]
    padding = [(0, 0)] * (source.ndim - 1)
    if offset > 0:
        moved_values = jnp.pad(source[..., offset:], padding + [(0, offset)])
    else:
        moved_values = jnp.pad(source[..., : length_last + offset], padding + [(-offset, 0)])
    return jnp.where(inside, moved_values, jnp.zeros_like(moved_values))


def diffusion(extended, conductance_ext, side_cells):
    center = extended[..., 1:-1, :]
    conduct = conductance_ext[1:-1]
    flux_sum = 0.5 * (conduct + conductance_ext[2:]) * (center - extended[..., 2:, :])
    flux_sum = flux_sum + 0.5 * (conduct + conductance_ext[:-2]) * (center - extended[..., :-2, :])
    column = lax.iota(jnp.int32, center.shape[-1]) % side_cells
    everywhere = column >= 0
    for offset, inside in (
        (1, column < side_cells - 1),
        (-1, column > 0),
        (side_cells, everywhere),
        (-side_cells, everywhere),
    ):
        flux_sum = flux_sum + 0.5 * (conduct + shifted(conduct, offset, inside)) * (
            center - shifted(center, offset, inside)
        )
    return flux_sum


def shards(panels, mean_field, fluctuations, products, triples, owner_slot):
    own_count = panels.shape[0]
    slot_count = own_count * lax.axis_size("chaos")
    coefficients = jnp.concatenate([mean_field[None], fluctuations], axis=0)
    field_count = coefficients.shape[0]
    padded_coef = padded(coefficients, (("space", 1),), 1)
    row_slot = owner_slot[triples[:, 0]]
    column_slot = owner_slot[triples[:, 1]]
    tables = (
        jnp.zeros((field_count, slot_count, slot_count), jnp.float32)
        .at[triples[:, 2], row_slot, column_slot]
        .add(products)
    )
    tables = tables.astype(jnp.bfloat16)
    own_tables = lax.dynamic_slice_in_dim(tables, lax.axis_index("chaos") * own_count, own_count, 1)

    def combine(own_panels):
        summed = jnp.einsum(
            "krc,cpv->krpv",
            own_tables,
            lax.all_gather(own_panels, "chaos", axis=0, tiled=True),
            preferred_element_type=jnp.float32,
        )
        return summed.astype(jnp.bfloat16)

    def galerkin_apply(own_panels):
        combined = padded(combine(own_panels), (("space", 2),), 1)
        combined = lax.optimization_barrier(combined)
        result = jnp.zeros(own_panels.shape, jnp.float32)
        for field_index in range(field_count):
            result = result + diffusion(
                combined[field_index].astype(jnp.float32), padded_coef[field_index], NXY
            )
        return (scale_factor * result).astype(jnp.bfloat16)

    first_values = galerkin_apply(panels)
    second_values = galerkin_apply(first_values)
    return (first_values, second_values)


def solution(mesh):
    in_specs = (P("chaos", "space", None), P("space", None), P(None, "space", None), P(), P(), P())
    out_specs = (P("chaos", "space", None), P("chaos", "space", None))
    return jax.shard_map(shards, mesh=mesh, in_specs=in_specs, out_specs=out_specs, check_vma=False)
```

profile of v0, /device:TPU:6, one launch (start us, length us, event | category | flops | bytes accessed | tf_op | source)
XLA Modules:
  0.0 220.9 jit_solution(4822046470193139959)
XLA Ops:
  8.5 5.2 %collective-permute-start = (f32[7,1,2304]{2,1,0:T(1,128)S(1)}, f32[7,1,2304]{2,1,0:T(1,128)S(1)}, u32[]{:S(2)}, u32[]{:S(2)}) collective-permute-start(f32[7,1,2304]{2,1,0:T(1,128)S(1)} %get-tuple-element.94), channel_id=1, source_target_pairs={{1,0},{2,1},{3,2},{4,3},{5,4},{6,5},{7,6},{8,7},{9,8},{10,9},{11,1... | collective-permute-start | bytes 193544 | tf_op jit(solution)/shard_map/ppermute | solution.py:18
  13.7 1.9 collective-permute-start.3
  15.6 2.1 copy.8
  18.1 8.0 %gather_fusion.1 = s32[1218]{0:T(1024)S(1)} fusion(s32[210]{0:T(256)S(1)} %copy-done, s32[2048]{0:T(1024)S(1)} %get-tuple-element.162), kind=kCustom, calls=%fused_computation.1 | custom fusion | bytes 14616 | tf_op jit(solution)/shard_map/gather | solution.py:59
  26.1 8.0 %gather_fusion = s32[1218]{0:T(1024)S(1)} fusion(s32[210]{0:T(256)S(1)} %copy-done, s32[2048]{0:T(1024)S(1)} %get-tuple-element.163), kind=kCustom, calls=%fused_computation | custom fusion | bytes 14616 | tf_op jit(solution)/shard_map/gather | solution.py:58
  34.3 7.8 %scatter_custom_fusion = f32[326592]{0:T(1024)S(1)} fusion(s32[1218]{0:T(1024)S(1)} %broadcast_select_fusion, f32[1218]{0:T(1024)} %param.9, f32[]{:T(128)} %constant.69.clone.1), kind=kCustom, calls=%fused_computation.181 | custom fusion | flops 1218 | bytes 1306880
  42.2 2.5 %reshape.112 = bf16[7,216,216]{2,1,0:T(8,128)(2,1)S(1)} reshape(bf16[326592]{0:T(1024)(128)(2,1)S(1)} %convert_element_type.252) | data formatting | bytes 1306368 | tf_op jit(solution)/shard_map/convert_element_type | solution.py:65
  49.5 2.7 %all-gather.3.cloned.1.call-done = bf16[216,3,2304]{2,1,0:T(4,128)(2,1)} async-done(((bf16[27,3,2304]{2,1,0:T(4,128)(2,1)}), bf16[216,3,2304]{2,1,0:T(4,128)(2,1)}) %all-gather.3.cloned.1.call-update) | async-done | bytes 2986000 | tf_op jit(solution)/shard_map/all_gather | solution.py:72
  52.2 3.1 %convolution_convert_fusion.1 = bf16[7,27,3,2304]{3,1,2,0:T(8,128)(2,1)S(1)} fusion(bf16[216,3,2304]{2,1,0:T(4,128)(2,1)} %all-gather.3.cloned.1.call-done, bf16[7,216,216]{2,1,0:T(8,128)(2,1)S(1)} %reshape.112, s32[]{:T(128)S(6)} %select_n.521), kind=kOutput, calls=%fused_computation.6 | convolution fusion | flops 565657344 | bytes 5713412 | tf_op jit(solution)/shard_map/krc,cpv->krpv/dot_general | solution.py:69
  56.6 4.9 %collective-permute-start.2 = (bf16[7,27,1,2304]{3,0,2,1:T(8,128)(2,1)S(1)}, bf16[7,27,1,2304]{3,0,2,1:T(8,128)(2,1)S(1)}, u32[]{:S(2)}, u32[]{:S(2)}) collective-permute-start(bf16[7,27,1,2304]{3,0,2,1:T(8,128)(2,1)S(1)} %copy.11), channel_id=1, source_target_pairs={{1,0},{2,1},{3,2},{4,3},{5,4},{6,5},{7,6},{8,7},{9,8},{10,9},{11,1... | collective-permute-start | bytes 2612744 | tf_op jit(solution)/shard_map/ppermute | solution.py:18
  61.5 2.1 collective-permute-start.1
  64.6 18.6 %collective-permute-done.2 = bf16[7,27,1,2304]{3,0,2,1:T(8,128)(2,1)S(1)} collective-permute-done((bf16[7,27,1,2304]{3,0,2,1:T(8,128)(2,1)S(1)}, bf16[7,27,1,2304]{3,0,2,1:T(8,128)(2,1)S(1)}, u32[]{:S(2)}, u32[]{:S(2)}) %collective-permute-start.2) | collective-permute-done | bytes 870944 | tf_op jit(solution)/shard_map/ppermute | solution.py:18
  83.3 6.1 %collective-permute-done.1 = bf16[7,27,1,2304]{3,0,2,1:T(8,128)(2,1)S(1)} collective-permute-done((bf16[7,27,1,2304]{3,0,2,1:T(8,128)(2,1)S(1)}, bf16[7,27,1,2304]{3,0,2,1:T(8,128)(2,1)S(1)}, u32[]{:S(2)}, u32[]{:S(2)}) %collective-permute-start.1) | collective-permute-done | bytes 870944 | tf_op jit(solution)/shard_map/ppermute | solution.py:15
  100.9 1.6 fusion.197
  105.5 12.3 %fusion.69 = bf16[27,3,2304]{2,0,1:T(8,128)(2,1)} fusion(f32[27,5,2304]{2,0,1:T(8,128)S(1)} %get-tuple-element.12, f32[27,5,2304]{2,0,1:T(8,128)S(1)} %get-tuple-element.13, f32[27,5,2304]{2,0,1:T(8,128)S(1)} %get-tuple-element.14, f32[27,5,2304]{2,0,1:T(8,128)S(1)} %get-tuple-element.15, f32[27,5,2304]{2,0,1:T(8,128)S(1)} %get-tuple-element.16, ...), kind=kLoop, calls=%fused_computation.91 | loop fusion | flops 28926720 | bytes 37897416 | tf_op jit(solution)/shard_map/convert_element_type | solution.py:85
  117.8 2.1 copy.14
  119.9 28.6 %all-gather.5.cloned.1.call-done = bf16[216,3,2304]{2,1,0:T(4,128)(2,1)} async-done(((bf16[27,3,2304]{2,1,0:T(4,128)(2,1)}), bf16[216,3,2304]{2,1,0:T(4,128)(2,1)}) %all-gather.5.cloned.1.call-update) | async-done | bytes 2986000 | tf_op jit(solution)/shard_map/all_gather | solution.py:72
  148.5 3.2 %convolution_convert_fusion = bf16[7,27,3,2304]{3,1,2,0:T(8,128)(2,1)S(1)} fusion(bf16[216,3,2304]{2,1,0:T(4,128)(2,1)} %all-gather.5.cloned.1.call-done, bf16[7,216,216]{2,1,0:T(8,128)(2,1)} %copy-done.4, s32[]{:T(128)S(6)} %select_n.521), kind=kOutput, calls=%fused_computation.5 | convolution fusion | flops 565657344 | bytes 6708740 | tf_op jit(solution)/shard_map/krc,cpv->krpv/dot_general | solution.py:69
  152.4 4.9 %collective-permute-start.5 = (bf16[7,27,1,2304]{3,0,2,1:T(8,128)(2,1)S(1)}, bf16[7,27,1,2304]{3,0,2,1:T(8,128)(2,1)S(1)}, u32[]{:S(2)}, u32[]{:S(2)}) collective-permute-start(bf16[7,27,1,2304]{3,0,2,1:T(8,128)(2,1)S(1)} %copy.17), channel_id=1, source_target_pairs={{1,0},{2,1},{3,2},{4,3},{5,4},{6,5},{7,6},{8,7},{9,8},{10,9},{11,1... | collective-permute-start | bytes 2612744 | tf_op jit(solution)/shard_map/ppermute | solution.py:18
  157.8 2.1 collective-permute-start.4
  160.0 19.0 %collective-permute-done.5 = bf16[7,27,1,2304]{3,0,2,1:T(8,128)(2,1)S(1)} collective-permute-done((bf16[7,27,1,2304]{3,0,2,1:T(8,128)(2,1)S(1)}, bf16[7,27,1,2304]{3,0,2,1:T(8,128)(2,1)S(1)}, u32[]{:S(2)}, u32[]{:S(2)}) %collective-permute-start.5) | collective-permute-done | bytes 870944 | tf_op jit(solution)/shard_map/ppermute | solution.py:18
  179.1 6.6 %collective-permute-done.4 = bf16[7,27,1,2304]{3,0,2,1:T(8,128)(2,1)S(1)} collective-permute-done((bf16[7,27,1,2304]{3,0,2,1:T(8,128)(2,1)S(1)}, bf16[7,27,1,2304]{3,0,2,1:T(8,128)(2,1)S(1)}, u32[]{:S(2)}, u32[]{:S(2)}) %collective-permute-start.4) | collective-permute-done | bytes 870944 | tf_op jit(solution)/shard_map/ppermute | solution.py:15
  197.2 1.6 fusion.183
  201.8 12.3 %fusion.12 = bf16[27,3,2304]{2,0,1:T(8,128)(2,1)} fusion(f32[27,5,2304]{2,0,1:T(8,128)S(1)} %get-tuple-element.5, f32[27,5,2304]{2,0,1:T(8,128)S(1)} %get-tuple-element.6, f32[27,5,2304]{2,0,1:T(8,128)S(1)} %get-tuple-element.7, f32[27,5,2304]{2,0,1:T(8,128)S(1)} %get-tuple-element.8, f32[27,5,2304]{2,0,1:T(8,128)S(1)} %get-tuple-element.9, ...), kind=kLoop, calls=%fused_computation.20 | loop fusion | flops 28926720 | bytes 37897416 | tf_op jit(solution)/shard_map/convert_element_type | solution.py:85
  (88 shorter events, 39.1 us)
Async XLA Ops:
  7.2 10.9 %copy-start = (s32[210]{0:T(256)S(1)}, s32[210]{0:T(256)}, u32[]{:S(2)}) copy-start(s32[210]{0:T(256)} %param.11) | copy-start | bytes 2524
  7.2 10.6 %copy-start.3 = (f32[3,2304]{1,0:T(4,128)S(1)}, f32[3,2304]{1,0:T(4,128)}, u32[]{:S(2)}) copy-start(f32[3,2304]{1,0:T(4,128)} %param.7) | copy-start | bytes 82948
  7.2 10.8 %copy-start.5 = (s32[1218,3]{0,1:T(4,128)S(1)}, s32[1218,3]{0,1:T(4,128)}, u32[]{:S(2)}) copy-start(s32[1218,3]{0,1:T(4,128)} %param.10) | copy-start | bytes 43852
  7.2 45.0 %all-gather.3.cloned.1.call-start = ((), (), s32[]{:S(2)}) async-start(), calls=%async_computation | async-start | bytes 4478976 | tf_op jit(solution)/shard_map/all_gather | solution.py:72
  8.5 36.3 %collective-permute-start = (f32[7,1,2304]{2,1,0:T(1,128)S(1)}, f32[7,1,2304]{2,1,0:T(1,128)S(1)}, u32[]{:S(2)}, u32[]{:S(2)}) collective-permute-start(f32[7,1,2304]{2,1,0:T(1,128)S(1)} %get-tuple-element.94), channel_id=1, source_target_pairs={{1,0},{2,1},{3,2},{4,3},{5,4},{6,5},{7,6},{8,7},{9,8},{10,9},{11,1... | collective-permute-start | bytes 193544 | tf_op jit(solution)/shard_map/ppermute | solution.py:18
  13.7 31.1 %collective-permute-start.3 = (f32[7,1,2304]{2,1,0:T(1,128)S(1)}, f32[7,1,2304]{2,1,0:T(1,128)S(1)}, u32[]{:S(2)}, u32[]{:S(2)}) collective-permute-start(f32[7,1,2304]{2,1,0:T(1,128)S(1)} %get-tuple-element.95), channel_id=1, source_target_pairs={{0,1},{1,2},{2,3},{3,4},{4,5},{5,6},{6,7},{7,8},{8,9},{9,10},{10,1... | collective-permute-start | bytes 193544 | tf_op jit(solution)/shard_map/ppermute | solution.py:15
  17.7 130.7 %all-gather.5.cloned.1.call-start = ((), (), s32[]{:S(2)}) async-start(), calls=%async_computation.1 | async-start | bytes 4478976 | tf_op jit(solution)/shard_map/all_gather | solution.py:72
  26.1 8.0 %copy-start.7 = (s32[3]{0:T(128)S(1)}, s32[3]{0:T(128)}, u32[]{:S(2)}) copy-start(s32[3]{0:T(128)} %constant.254) | copy-start | bytes 40
  26.1 8.1 %copy-start.6 = (s32[3]{0:T(128)S(1)}, s32[3]{0:T(128)}, u32[]{:S(2)}) copy-start(s32[3]{0:T(128)} %constant.251) | copy-start | bytes 40
  42.1 2.7 %copy-start.2 = (f32[6,3,2304]{2,1,0:T(4,128)S(1)}, f32[6,3,2304]{2,1,0:T(4,128)}, u32[]{:S(2)}) copy-start(f32[6,3,2304]{2,1,0:T(4,128)} %param.8) | copy-start | bytes 497668
  44.7 7.5 %copy-start.4 = (bf16[7,216,216]{2,1,0:T(8,128)(2,1)}, bf16[7,216,216]{2,1,0:T(8,128)(2,1)S(1)}, u32[]{:S(2)}) copy-start(bf16[7,216,216]{2,1,0:T(8,128)(2,1)S(1)} %reshape.112) | copy-start | bytes 1959556
  56.6 26.6 %collective-permute-start.2 = (bf16[7,27,1,2304]{3,0,2,1:T(8,128)(2,1)S(1)}, bf16[7,27,1,2304]{3,0,2,1:T(8,128)(2,1)S(1)}, u32[]{:S(2)}, u32[]{:S(2)}) collective-permute-start(bf16[7,27,1,2304]{3,0,2,1:T(8,128)(2,1)S(1)} %copy.11), channel_id=1, source_target_pairs={{1,0},{2,1},{3,2},{4,3},{5,4},{6,5},{7,6},{8,7},{9,8},{10,9},{11,1... | collective-permute-start | bytes 2612744 | tf_op jit(solution)/shard_map/ppermute | solution.py:18
  61.5 27.9 %collective-permute-start.1 = (bf16[7,27,1,2304]{3,0,2,1:T(8,128)(2,1)S(1)}, bf16[7,27,1,2304]{3,0,2,1:T(8,128)(2,1)S(1)}, u32[]{:S(2)}, u32[]{:S(2)}) collective-permute-start(bf16[7,27,1,2304]{3,0,2,1:T(8,128)(2,1)S(1)} %copy.10), channel_id=1, source_target_pairs={{0,1},{1,2},{2,3},{3,4},{4,5},{5,6},{6,7},{7,8},{8,9},{9,10},{10,1... | collective-permute-start | bytes 2612744 | tf_op jit(solution)/shard_map/ppermute | solution.py:15
  152.4 26.6 %collective-permute-start.5 = (bf16[7,27,1,2304]{3,0,2,1:T(8,128)(2,1)S(1)}, bf16[7,27,1,2304]{3,0,2,1:T(8,128)(2,1)S(1)}, u32[]{:S(2)}, u32[]{:S(2)}) collective-permute-start(bf16[7,27,1,2304]{3,0,2,1:T(8,128)(2,1)S(1)} %copy.17), channel_id=1, source_target_pairs={{1,0},{2,1},{3,2},{4,3},{5,4},{6,5},{7,6},{8,7},{9,8},{10,9},{11,1... | collective-permute-start | bytes 2612744 | tf_op jit(solution)/shard_map/ppermute | solution.py:18
  157.8 27.9 %collective-permute-start.4 = (bf16[7,27,1,2304]{3,0,2,1:T(8,128)(2,1)S(1)}, bf16[7,27,1,2304]{3,0,2,1:T(8,128)(2,1)S(1)}, u32[]{:S(2)}, u32[]{:S(2)}) collective-permute-start(bf16[7,27,1,2304]{3,0,2,1:T(8,128)(2,1)S(1)} %copy.16), channel_id=1, source_target_pairs={{0,1},{1,2},{2,3},{3,4},{4,5},{5,6},{6,7},{7,8},{8,9},{9,10},{10,1... | collective-permute-start | bytes 2612744 | tf_op jit(solution)/shard_map/ppermute | solution.py:15
  201.8 12.3 %copy-start.1 = (s32[210]{0:T(256)S(1)}, s32[210]{0:T(256)}, u32[]{:S(2)}) copy-start(s32[210]{0:T(256)} %param.11) | copy-start | bytes 2524
Sparse Core Ops, SparseCore 0:
  17.8 34.3 all-gather.2
  120.0 28.4 all-gather.4
where the time goes:
time: 221 us
  waiting for transfers between devices  81.5 us (37%)
  local copies, waits for them, and re-layouts  54.2 us (25%)
  other arithmetic  43 us (19%)
  starting transfers between devices  21.3 us (10%)
  between operations  14.5 us (7%)
  matrix products  6.38 us (3%)
    ppermute x3, waiting for transfers between devices, padded(): lax.ppermute(lax.slice_in_dim(block, 0, width, axis=dim), axis, backward)  37.6 us
    all_gather x2, waiting for transfers between devices, combine(): lax.all_gather(own_panels, 'chaos', axis=0, tiled=True)  31.3 us
    slice x36, local copies, waits for them, and re-layouts, shifted(): moved_values = jnp.pad(source[..., offset:], padding + [(0, offset)])  28.5 us
    convert_element_type x2, other arithmetic, galerkin_apply(): return (scale_factor * result).astype(jnp.bfloat16)  24.6 us
    ppermute x3, starting transfers between devices, padded(): lax.ppermute(lax.slice_in_dim(block, 0, width, axis=dim), axis, backward)  15.1 us
    ppermute x3, waiting for transfers between devices, padded(): lax.ppermute(lax.slice_in_dim(block, block.shape[dim] - width, None, axis...  12.6 us
    gather x1, local copies, waits for them, and re-layouts, shards(): column_slot = owner_slot[triples[:, 1]]  7.98 us
    gather x1, local copies, waits for them, and re-layouts, shards(): row_slot = owner_slot[triples[:, 0]]  7.98 us
  transfers between devices with their start and end apart: 8, of which 6 were waited for; matrix products, arithmetic and copies ran while one was open for 16% of the time, Pallas kernels for 0%

commit v1 on v0

--- a/solution.py
+++ b/solution.py
@@ -69,7 +69,10 @@
         summed = jnp.einsum(
             "krc,cpv->krpv",
             own_tables,
-            lax.all_gather(own_panels, "chaos", axis=0, tiled=True),
+            jnp.concatenate(
+                lax.all_to_all(jnp.stack([own_panels] * lax.axis_size("chaos")), "chaos", 0, 0),
+                axis=0,
+            ),
             preferred_element_type=jnp.float32,
         )
         return summed.astype(jnp.bfloat16)

time: 221 us -> 258 us (1.17)
  blocking collectives: 0 us -> 46.9 us
  waiting for transfers between devices: 81.5 us -> 48 us
  local copies, waits for them, and re-layouts: 54.2 us -> 74.6 us
  between operations: 14.5 us -> 1.28 us
  other arithmetic: 43 us -> 54.6 us
  starting transfers between devices: 21.3 us -> 26.6 us
    all_to_all x0 -> x1, blocking collectives: none -> 46.9 us  [combine(): lax.all_to_all(jnp.stack([own_panels] * lax.axis_size('chaos')), 'chaos',...]
    all_gather x2 -> x0, waiting for transfers between devices: 31.3 us -> none  [combine(): lax.all_gather(own_panels, 'chaos', axis=0, tiled=True)]
    reshape x0 -> x2, local copies, waits for them, and re-layouts: none -> 5.88 us  [combine(): jnp.concatenate(lax.all_to_all(jnp.stack([own_panels] * lax.axis_size('ch...]
    all_to_all x0 -> x1, starting transfers between devices: none -> 5.31 us  [combine(): lax.all_to_all(jnp.stack([own_panels] * lax.axis_size('chaos')), 'chaos',...]
    another operation x0 -> x2, local copies, waits for them, and re-layouts: none -> 4.53 us  [combine(): jnp.stack([own_panels] * lax.axis_size('chaos'))]
    slice x36, local copies, waits for them, and re-layouts: 28.5 us -> 32.7 us  [shifted(): moved_values = jnp.pad(source[..., offset:], padding + [(0, offset)])]
    gather x1, local copies, waits for them, and re-layouts: 7.98 us -> 11.1 us  [shards(): row_slot = owner_slot[triples[:, 0]]]
    gather x1, local copies, waits for them, and re-layouts: 7.98 us -> 10.9 us  [shards(): column_slot = owner_slot[triples[:, 1]]]
  transfers between devices with their start and end apart: 8 -> 7, of which waited for: 6 -> 4; matrix products, arithmetic and copies ran while one was open for 16% -> 23% of each run, Pallas kernels for 0% -> 0%
where the time goes in v1:
time: 258 us; the launch traced here: 257 us
  local copies, waits for them, and re-layouts  74.6 us (29%)
  other arithmetic  54.6 us (21%)
  waiting for transfers between devices  48 us (19%)
  blocking collectives  46.9 us (18%)
  starting transfers between devices  26.6 us (10%)
  matrix products  4.79 us (2%)
    all_to_all x1, blocking collectives, combine(): lax.all_to_all(jnp.stack([own_panels] * lax.axis_size('chaos')), 'chaos',...  46.9 us
    ppermute x3, waiting for transfers between devices, padded(): lax.ppermute(lax.slice_in_dim(block, 0, width, axis=dim), axis, backward)  37.6 us
    slice x36, local copies, waits for them, and re-layouts, shifted(): moved_values = jnp.pad(source[..., offset:], padding + [(0, offset)])  32.7 us
    convert_element_type x2, other arithmetic, galerkin_apply(): return (scale_factor * result).astype(jnp.bfloat16)  24.5 us
    ppermute x3, starting transfers between devices, padded(): lax.ppermute(lax.slice_in_dim(block, 0, width, axis=dim), axis, backward)  13.1 us
    gather x1, local copies, waits for them, and re-layouts, shards(): row_slot = owner_slot[triples[:, 0]]  11.1 us
    gather x1, local copies, waits for them, and re-layouts, shards(): column_slot = owner_slot[triples[:, 1]]  10.9 us
    unnamed x4, other arithmetic  10.8 us
  transfers between devices with their start and end apart: 7, of which 4 were waited for; matrix products, arithmetic and copies ran while one was open for 23% of the time, Pallas kernels for 0%

profile of v1, /device:TPU:6, one launch (start us, length us, event | category | flops | bytes accessed | tf_op | source)
XLA Modules:
  0.0 256.8 jit_solution(1679194752362369505)
XLA Ops:
  2.5 5.2 %collective-permute-start = (f32[7,1,2304]{2,1,0:T(1,128)}, f32[7,1,2304]{2,1,0:T(1,128)}, u32[]{:S(2)}, u32[]{:S(2)}) collective-permute-start(f32[7,1,2304]{2,1,0:T(1,128)} %get-tuple-element.94), channel_id=1, source_target_pairs={{1,0},{2,1},{3,2},{4,3},{5,4},{6,5},{7,6},{8,7},{9,8},{10,9},{11,1... | collective-permute-start | bytes 193544 | tf_op jit(solution)/shard_map/ppermute | solution.py:18
  7.7 1.9 collective-permute-start.3
  9.6 3.1 %stack.4 = bf16[8,27,3,2304]{3,1,2,0:T(8,128)(2,1)} broadcast(bf16[27,3,2304]{2,0,1:T(8,128)(2,1)} %param.6), dimensions={1,2,3} | broadcast | bytes 3359232 | tf_op jit(solution)/shard_map/stack | solution.py:73
  12.8 5.3 %all-to-all-start = ((bf16[8,27,3,2304]{3,1,2,0:T(8,128)(2,1)}), bf16[8,27,3,2304]{3,1,2,0:T(8,128)(2,1)S(1)}, u32[]{:S(2)}, u32[]{:S(2)}) async-start(bf16[8,27,3,2304]{3,1,2,0:T(8,128)(2,1)} %stack.4), calls=%async_computation | async-start | bytes 7077888 | tf_op jit(solution)/shard_map/all_to_all | solution.py:73
  23.2 10.9 %gather_fusion.1 = s32[1218]{0:T(1024)} fusion(s32[210]{0:T(256)S(1)} %copy-done, s32[2048]{0:T(1024)} %get-tuple-element.162), kind=kCustom, calls=%fused_computation.1 | custom fusion | bytes 14616 | tf_op jit(solution)/shard_map/gather | solution.py:59
  35.5 11.1 %gather_fusion = s32[1218]{0:T(1024)} fusion(s32[210]{0:T(256)S(1)} %copy-done, s32[2048]{0:T(1024)} %get-tuple-element.163), kind=kCustom, calls=%fused_computation | custom fusion | bytes 14616 | tf_op jit(solution)/shard_map/gather | solution.py:58
  49.4 8.5 %scatter_custom_fusion = f32[326592]{0:T(1024)} fusion(s32[1218]{0:T(1024)} %broadcast_select_fusion, f32[1218]{0:T(1024)} %param.9, f32[]{:T(128)} %constant.69.clone.1), kind=kCustom, calls=%fused_computation.177 | custom fusion | flops 1218 | bytes 1306880
  58.0 2.2 convert_element_type.252
  60.2 4.2 %reshape.124 = bf16[7,216,216]{2,1,0:T(8,128)(2,1)} reshape(bf16[326592]{0:T(1024)(128)(2,1)} %convert_element_type.252) | data formatting | bytes 1306368 | tf_op jit(solution)/shard_map/convert_element_type | solution.py:65
  72.6 2.0 copy.8
  74.7 3.2 %reshape.162 = bf16[216,3,2304,1]{2,0,1,3:T(8,128)(2,1)S(1)} reshape(bf16[8,27,3,2304]{3,1,0,2:T(8,128)(2,1)} %copy.8) | data formatting | bytes 5971968 | tf_op jit(solution)/shard_map/reshape | solution.py:72
  81.1 6.0 %collective-permute-start.2 = (bf16[7,27,1,2304]{3,0,2,1:T(8,128)(2,1)S(1)}, bf16[7,27,1,2304]{3,0,2,1:T(8,128)(2,1)S(1)}, u32[]{:S(2)}, u32[]{:S(2)}) collective-permute-start(bf16[7,27,1,2304]{3,0,2,1:T(8,128)(2,1)S(1)} %copy.10), channel_id=1, source_target_pairs={{1,0},{2,1},{3,2},{4,3},{5,4},{6,5},{7,6},{8,7},{9,8},{10,9},{11,1... | collective-permute-start | bytes 2612744 | tf_op jit(solution)/shard_map/ppermute | solution.py:18
  87.1 2.1 collective-permute-start.1
  90.3 18.7 %collective-permute-done.2 = bf16[7,27,1,2304]{3,0,2,1:T(8,128)(2,1)S(1)} collective-permute-done((bf16[7,27,1,2304]{3,0,2,1:T(8,128)(2,1)S(1)}, bf16[7,27,1,2304]{3,0,2,1:T(8,128)(2,1)S(1)}, u32[]{:S(2)}, u32[]{:S(2)}) %collective-permute-start.2) | collective-permute-done | bytes 870944 | tf_op jit(solution)/shard_map/ppermute | solution.py:18
  109.2 6.1 %collective-permute-done.1 = bf16[7,27,1,2304]{3,0,2,1:T(8,128)(2,1)S(1)} collective-permute-done((bf16[7,27,1,2304]{3,0,2,1:T(8,128)(2,1)S(1)}, bf16[7,27,1,2304]{3,0,2,1:T(8,128)(2,1)S(1)}, u32[]{:S(2)}, u32[]{:S(2)}) %collective-permute-start.1) | collective-permute-done | bytes 870944 | tf_op jit(solution)/shard_map/ppermute | solution.py:15
  131.3 12.2 %fusion.65 = bf16[27,3,2304]{2,0,1:T(8,128)(2,1)} fusion(f32[27,5,2304]{2,0,1:T(8,128)S(1)} %get-tuple-element.12, f32[27,5,2304]{2,0,1:T(8,128)S(1)} %get-tuple-element.13, f32[27,5,2304]{2,0,1:T(8,128)S(1)} %get-tuple-element.14, f32[27,5,2304]{2,0,1:T(8,128)S(1)} %get-tuple-element.15, f32[27,5,2304]{2,0,1:T(8,128)S(1)} %get-tuple-element.16, ...), kind=kLoop, calls=%fused_computation.87 | loop fusion | flops 28926720 | bytes 37897416 | tf_op jit(solution)/shard_map/convert_element_type | solution.py:88
  145.0 46.9 %all_to_all.10 = bf16[8,27,3,2304]{3,1,2,0:T(8,128)(2,1)S(1)} all-to-all(bf16[8,27,3,2304]{3,1,2,0:T(8,128)(2,1)S(1)} %stack.5), channel_id=1, replica_groups=mesh['chaos'=8,'space'=16] {'chaos'}, dimensions={0} | all-to-all | bytes 5971968 | tf_op jit(solution)/shard_map/all_to_all | solution.py:73
  192.1 2.7 %reshape.163 = bf16[216,3,2304,1]{2,0,1,3:T(8,128)(2,1)} reshape(bf16[8,27,3,2304]{3,1,0,2:T(8,128)(2,1)S(1)} %copy.13) | data formatting | bytes 5971968 | tf_op jit(solution)/shard_map/reshape | solution.py:72
  194.8 2.9 %convolution_convert_fusion = bf16[7,27,3,2304]{3,1,2,0:T(8,128)(2,1)S(1)} fusion(bf16[216,3,2304,1]{2,0,1,3:T(8,128)(2,1)} %reshape.163, bf16[7,216,216]{2,1,0:T(8,128)(2,1)} %reshape.124, s32[]{:T(128)S(6)} %select_n.521), kind=kOutput, calls=%fused_computation.5 | convolution fusion | flops 565657344 | bytes 5713412 | tf_op jit(solution)/shard_map/krc,cpv->krpv/dot_general | solution.py:69
  198.3 1.9 collective-permute-start.5
  200.7 4.1 %collective-permute-start.4 = (bf16[7,27,1,2304]{3,0,2,1:T(8,128)(2,1)S(1)}, bf16[7,27,1,2304]{3,0,2,1:T(8,128)(2,1)S(1)}, u32[]{:S(2)}, u32[]{:S(2)}) collective-permute-start(bf16[7,27,1,2304]{3,0,2,1:T(8,128)(2,1)S(1)} %copy.14), channel_id=1, source_target_pairs={{0,1},{1,2},{2,3},{3,4},{4,5},{5,6},{6,7},{7,8},{8,9},{9,10},{10,1... | collective-permute-start | bytes 2612744 | tf_op jit(solution)/shard_map/ppermute | solution.py:15
  204.9 18.9 %collective-permute-done.5 = bf16[7,27,1,2304]{3,0,2,1:T(8,128)(2,1)S(1)} collective-permute-done((bf16[7,27,1,2304]{3,0,2,1:T(8,128)(2,1)S(1)}, bf16[7,27,1,2304]{3,0,2,1:T(8,128)(2,1)S(1)}, u32[]{:S(2)}, u32[]{:S(2)}) %collective-permute-start.5) | collective-permute-done | bytes 870944 | tf_op jit(solution)/shard_map/ppermute | solution.py:18
  223.9 4.4 %collective-permute-done.4 = bf16[7,27,1,2304]{3,0,2,1:T(8,128)(2,1)S(1)} collective-permute-done((bf16[7,27,1,2304]{3,0,2,1:T(8,128)(2,1)S(1)}, bf16[7,27,1,2304]{3,0,2,1:T(8,128)(2,1)S(1)}, u32[]{:S(2)}, u32[]{:S(2)}) %collective-permute-start.4) | collective-permute-done | bytes 870944 | tf_op jit(solution)/shard_map/ppermute | solution.py:15
  244.4 12.2 %fusion.8 = bf16[27,3,2304]{2,0,1:T(8,128)(2,1)} fusion(f32[27,5,2304]{2,0,1:T(8,128)S(1)} %get-tuple-element.5, f32[27,5,2304]{2,0,1:T(8,128)S(1)} %get-tuple-element.6, f32[27,5,2304]{2,0,1:T(8,128)S(1)} %get-tuple-element.7, f32[27,5,2304]{2,0,1:T(8,128)S(1)} %get-tuple-element.8, f32[27,5,2304]{2,0,1:T(8,128)S(1)} %get-tuple-element.9, ...), kind=kLoop, calls=%fused_computation.16 | loop fusion | flops 28926720 | bytes 37897416 | tf_op jit(solution)/shard_map/convert_element_type | solution.py:88
  (115 shorter events, 58.7 us)
Async XLA Ops:
  0.6 22.6 %copy-start = (s32[210]{0:T(256)S(1)}, s32[210]{0:T(256)}, u32[]{:S(2)}) copy-start(s32[210]{0:T(256)} %param.11) | copy-start | bytes 2524
  2.5 62.0 %collective-permute-start = (f32[7,1,2304]{2,1,0:T(1,128)}, f32[7,1,2304]{2,1,0:T(1,128)}, u32[]{:S(2)}, u32[]{:S(2)}) collective-permute-start(f32[7,1,2304]{2,1,0:T(1,128)} %get-tuple-element.94), channel_id=1, source_target_pairs={{1,0},{2,1},{3,2},{4,3},{5,4},{6,5},{7,6},{8,7},{9,8},{10,9},{11,1... | collective-permute-start | bytes 193544 | tf_op jit(solution)/shard_map/ppermute | solution.py:18
  7.7 56.8 %collective-permute-start.3 = (f32[7,1,2304]{2,1,0:T(1,128)}, f32[7,1,2304]{2,1,0:T(1,128)}, u32[]{:S(2)}, u32[]{:S(2)}) collective-permute-start(f32[7,1,2304]{2,1,0:T(1,128)} %get-tuple-element.95), channel_id=1, source_target_pairs={{0,1},{1,2},{2,3},{3,4},{4,5},{5,6},{6,7},{7,8},{8,9},{9,10},{10,1... | collective-permute-start | bytes 193544 | tf_op jit(solution)/shard_map/ppermute | solution.py:15
  12.8 59.9 %all-to-all-start = ((bf16[8,27,3,2304]{3,1,2,0:T(8,128)(2,1)}), bf16[8,27,3,2304]{3,1,2,0:T(8,128)(2,1)S(1)}, u32[]{:S(2)}, u32[]{:S(2)}) async-start(bf16[8,27,3,2304]{3,1,2,0:T(8,128)(2,1)} %stack.4), calls=%async_computation | async-start | bytes 7077888 | tf_op jit(solution)/shard_map/all_to_all | solution.py:73
  35.5 12.6 %copy-start.20 = (s32[3]{0:T(128)S(1)}, s32[3]{0:T(128)}, u32[]{:S(2)}) copy-start(s32[3]{0:T(128)} %constant.251) | copy-start | bytes 40
  64.4 4.0 %copy-start.2 = (f32[6,3,2304]{2,1,0:T(4,128)S(1)}, f32[6,3,2304]{2,1,0:T(4,128)}, u32[]{:S(2)}) copy-start(f32[6,3,2304]{2,1,0:T(4,128)} %param.8) | copy-start | bytes 497668
  64.4 4.0 %copy-start.4 = (f32[3,2304]{1,0:T(4,128)S(1)}, f32[3,2304]{1,0:T(4,128)}, u32[]{:S(2)}) copy-start(f32[3,2304]{1,0:T(4,128)} %param.7) | copy-start | bytes 82948
  67.5 3.4 %copy-start.5 = (f32[3,2304]{1,0:T(4,128)}, f32[3,2304]{1,0:T(4,128)S(1)}, u32[]{:S(2)}) copy-start(f32[3,2304]{1,0:T(4,128)S(1)} %get-tuple-element.122) | copy-start | bytes 82948
  67.6 3.4 %copy-start.7 = (f32[3,2304]{1,0:T(4,128)}, f32[3,2304]{1,0:T(4,128)S(1)}, u32[]{:S(2)}) copy-start(f32[3,2304]{1,0:T(4,128)S(1)} %get-tuple-element.123) | copy-start | bytes 82948
  68.4 3.4 %copy-start.11 = (f32[3,2303]{1,0:T(4,128)S(1)}, f32[3,2303]{1,0:T(4,128)}, u32[]{:S(2)}) copy-start(f32[3,2303]{1,0:T(4,128)} %get-tuple-element.129) | copy-start | bytes 82912
  68.4 3.4 %copy-start.12 = (f32[3,2303]{1,0:T(4,128)S(1)}, f32[3,2303]{1,0:T(4,128)}, u32[]{:S(2)}) copy-start(f32[3,2303]{1,0:T(4,128)} %get-tuple-element.130) | copy-start | bytes 82912
  80.5 8.7 %copy-start.6 = (f32[3,2304]{1,0:T(4,128)S(1)}, f32[3,2304]{1,0:T(4,128)}, u32[]{:S(2)}) copy-start(f32[3,2304]{1,0:T(4,128)} %copy-done.5) | copy-start | bytes 82948
  80.5 8.7 %copy-start.8 = (f32[3,2304]{1,0:T(4,128)S(1)}, f32[3,2304]{1,0:T(4,128)}, u32[]{:S(2)}) copy-start(f32[3,2304]{1,0:T(4,128)} %copy-done.7) | copy-start | bytes 82948
  80.5 8.9 %copy-start.3 = (f32[6,3,2304]{2,1,0:T(4,128)S(1)}, f32[6,3,2304]{2,1,0:T(4,128)}, u32[]{:S(2)}) copy-start(f32[6,3,2304]{2,1,0:T(4,128)} %param.8) | copy-start | bytes 497668
  80.5 8.8 %copy-start.15 = (f32[3,2256]{1,0:T(4,128)S(1)}, f32[3,2256]{1,0:T(4,128)}, u32[]{:S(2)}) copy-start(f32[3,2256]{1,0:T(4,128)} %get-tuple-element.136) | copy-start | bytes 81220
  80.5 8.8 %copy-start.16 = (f32[3,2256]{1,0:T(4,128)S(1)}, f32[3,2256]{1,0:T(4,128)}, u32[]{:S(2)}) copy-start(f32[3,2256]{1,0:T(4,128)} %get-tuple-element.137) | copy-start | bytes 81220
  80.5 8.8 %copy-start.17 = (f32[3,2256]{1,0:T(4,128)S(1)}, f32[3,2256]{1,0:T(4,128)}, u32[]{:S(2)}) copy-start(f32[3,2256]{1,0:T(4,128)} %get-tuple-element.166) | copy-start | bytes 81220
  80.5 8.8 %copy-start.18 = (f32[3,2256]{1,0:T(4,128)S(1)}, f32[3,2256]{1,0:T(4,128)}, u32[]{:S(2)}) copy-start(f32[3,2256]{1,0:T(4,128)} %get-tuple-element.167) | copy-start | bytes 81220
  80.5 8.8 %copy-start.19 = (f32[3,2256]{1,0:T(4,128)S(1)}, f32[3,2256]{1,0:T(4,128)}, u32[]{:S(2)}) copy-start(f32[3,2256]{1,0:T(4,128)} %get-tuple-element.152) | copy-start | bytes 81220
  81.1 28.0 %collective-permute-start.2 = (bf16[7,27,1,2304]{3,0,2,1:T(8,128)(2,1)S(1)}, bf16[7,27,1,2304]{3,0,2,1:T(8,128)(2,1)S(1)}, u32[]{:S(2)}, u32[]{:S(2)}) collective-permute-start(bf16[7,27,1,2304]{3,0,2,1:T(8,128)(2,1)S(1)} %copy.10), channel_id=1, source_target_pairs={{1,0},{2,1},{3,2},{4,3},{5,4},{6,5},{7,6},{8,7},{9,8},{10,9},{11,1... | collective-permute-start | bytes 2612744 | tf_op jit(solution)/shard_map/ppermute | solution.py:18
  87.1 28.1 %collective-permute-start.1 = (bf16[7,27,1,2304]{3,0,2,1:T(8,128)(2,1)S(1)}, bf16[7,27,1,2304]{3,0,2,1:T(8,128)(2,1)S(1)}, u32[]{:S(2)}, u32[]{:S(2)}) collective-permute-start(bf16[7,27,1,2304]{3,0,2,1:T(8,128)(2,1)S(1)} %copy.9), channel_id=1, source_target_pairs={{0,1},{1,2},{2,3},{3,4},{4,5},{5,6},{6,7},{7,8},{8,9},{9,10},{10,1... | collective-permute-start | bytes 2612744 | tf_op jit(solution)/shard_map/ppermute | solution.py:15
  198.3 25.5 %collective-permute-start.5 = (bf16[7,27,1,2304]{3,0,2,1:T(8,128)(2,1)S(1)}, bf16[7,27,1,2304]{3,0,2,1:T(8,128)(2,1)S(1)}, u32[]{:S(2)}, u32[]{:S(2)}) collective-permute-start(bf16[7,27,1,2304]{3,0,2,1:T(8,128)(2,1)S(1)} %copy.15), channel_id=1, source_target_pairs={{1,0},{2,1},{3,2},{4,3},{5,4},{6,5},{7,6},{8,7},{9,8},{10,9},{11,1... | collective-permute-start | bytes 2612744 | tf_op jit(solution)/shard_map/ppermute | solution.py:18
  200.7 27.6 %collective-permute-start.4 = (bf16[7,27,1,2304]{3,0,2,1:T(8,128)(2,1)S(1)}, bf16[7,27,1,2304]{3,0,2,1:T(8,128)(2,1)S(1)}, u32[]{:S(2)}, u32[]{:S(2)}) collective-permute-start(bf16[7,27,1,2304]{3,0,2,1:T(8,128)(2,1)S(1)} %copy.14), channel_id=1, source_target_pairs={{0,1},{1,2},{2,3},{3,4},{4,5},{5,6},{6,7},{7,8},{8,9},{9,10},{10,1... | collective-permute-start | bytes 2612744 | tf_op jit(solution)/shard_map/ppermute | solution.py:15
  244.4 12.2 %copy-start.1 = (s32[210]{0:T(256)S(1)}, s32[210]{0:T(256)}, u32[]{:S(2)}) copy-start(s32[210]{0:T(256)} %param.11) | copy-start | bytes 2524
  (4 other events, 9.9 us)
